TPU v7x, 32 devices: a whole 2x2x4 slice. The times are simulated.
32 devices in a mesh: past: 4 (over y, x), second: 8 (over z, core).
Axes of the slice: x: 2, y: 2, z: 4, core: 2. Of those that a mesh axis runs over, the one named last changes fastest.
Arguments:
- resident: bfloat16 [12288, 12288], P('past', 'second'), may hold values from -6 to 6
- memory: bfloat16 [2, 384, 12288], P(None, None, 'past'), may hold values from -0.0546875 to 0.0546875
- previous: bfloat16 [2, 384, 12288], P(None, None, 'second'), may hold values from -6 to 6
- inverse_part: float32 [2, 384, 384], replicated, may hold values from -0.3125 to 0.3125
- pair_coupling: float32 [32, 32], replicated, may hold values from 0.0004510549 to 0.004510549
Outputs:
- fronts: bfloat16 [2, 384, 12288], P(None, None, 'second')
All inputs are finite; a program needn't handle non-finite values.
Results may differ from a plain program's by a relative error of at most 0.017.
Values may be sent and summed in bfloat16 or wider, within the bound.
A program may use at most 128 MiB of HBM per device.

v0:
```python
import jax
import jax.numpy as jnp
from jax import lax
from jax.sharding import PartitionSpec as P

step_size = 0.5


def orbital_flip(block, orbitals):
    row_count, col_count = block.shape
    blocks = block.reshape(row_count // orbitals, orbitals, col_count // orbitals, orbitals)
    return blocks.transpose(0, 3, 2, 1).reshape(row_count, col_count)


def solve_front(summed, prior, inverse_block):
    source = prior.astype(jnp.float32) - step_size * summed
    solved = source + jnp.dot(
        inverse_block, source, precision=lax.Precision.HIGHEST, preferred_element_type=jnp.float32
    )
    return solved.astype(jnp.bfloat16)


def self_energy(front, pair_coupling):
    orbitals = pair_coupling.shape[0]
    row_count, col_count = front.shape
    values = front.astype(jnp.float32)
    mirror = orbital_flip(values, orbitals)
    blocks = (values * values * mirror).reshape(
        row_count // orbitals, orbitals, col_count // orbitals, orbitals
    )
    return (
        (blocks * pair_coupling[None, :, None, :])
        .reshape(row_count, col_count)
        .astype(jnp.bfloat16)
    )


def per_device(resident, memory, previous, inverse_part, pair_coupling):
    past_count = lax.axis_size("past")

    def advance(memory_row, front_index):
        partial_value = jnp.dot(memory_row, resident, preferred_element_type=jnp.float32)
        summed = lax.psum(partial_value.astype(jnp.bfloat16), "past").astype(jnp.float32)
        prior_cols = previous[front_index]
        return solve_front(summed, prior_cols, inverse_part[front_index])

    front_one = advance(memory[0], 0)
    energy_one = self_energy(front_one, pair_coupling)
    band = energy_one.shape[0] // past_count
    own_rows = lax.dynamic_slice_in_dim(energy_one, lax.axis_index("past") * band, band, 0)
    wide_band = lax.all_gather(own_rows, "second", axis=1, tiled=True)
    gathered = lax.all_to_all(wide_band, "past", split_axis=1, concat_axis=0, tiled=True)
    orbitals = pair_coupling.shape[0]
    memory_next = (
        memory[1].astype(jnp.float32) + orbital_flip(gathered, orbitals).astype(jnp.float32)
    ).astype(jnp.bfloat16)
    front_two = advance(memory_next, 1)
    return jnp.stack([front_one, front_two])


def solution(mesh):
    in_specs = (P("past", "second"), P(None, None, "past"), P(None, None, "second"), P(), P())
    out_specs = P(None, None, "second")
    return jax.shard_map(
        per_device, mesh=mesh, in_specs=in_specs, out_specs=out_specs, check_vma=False
    )
```

profile of v0, /device:TPU:0, one launch (start us, length us, event | category | flops | bytes accessed | tf_op | source)
XLA Modules:
  0.0 301.7 jit_solution(1481439341360291000)
XLA Ops:
  6.5 0.0 copy-start
  6.5 0.0 all-reduce.3.cloned.1.call-start
  6.5 9.2 %convolution_convert_fusion.1 = bf16[384,1536]{1,0:T(8,128)(2,1)} fusion(bf16[3072,1536]{1,0:T(8,128)(2,1)} %param.5, bf16[2,384,3072]{2,1,0:T(8,128)(2,1)} %param.6), kind=kOutput, calls=%fused_computation.10 | convolution fusion | flops 3624468480 | bytes 12976128 | tf_op jit(solution)/shard_map/dot_general | solution.py:42
  15.8 0.0 all-reduce.3.cloned.1.call-update
  15.8 0.0 all-gather.2.cloned.1.call-start
  15.8 0.0 copy-done
  15.9 4.4 %mul.29 = f32[12,32,48,32]{3,2,1,0:T(8,128)} broadcast(f32[32,32]{1,0:T(8,128)S(1)} %copy-done), dimensions={1,3} | broadcast | bytes 2363392 | tf_op jit(solution)/shard_map/mul | solution.py:32
  20.3 6.9 %mul.30 = f32[384,1536]{1,0:T(8,128)S(1)} reshape(f32[12,32,48,32]{3,2,1,0:T(8,128)} %mul.29) | data formatting | bytes 4718592 | tf_op jit(solution)/shard_map/mul | solution.py:32
  27.2 45.8 %all-reduce.3.cloned.1.call-done = bf16[384,1536]{1,0:T(8,128)(2,1)} async-done(((bf16[384,1536]{1,0:T(8,128)(2,1)}), bf16[384,1536]{1,0:T(8,128)(2,1)}) %all-reduce.3.cloned.1.call-update) | async-done | bytes 1179664 | tf_op jit(solution)/shard_map/psum | solution.py:43
  73.0 8.3 %fusion.28 = (f32[384,1536]{1,0:T(8,128)}, bf16[384,1536]{1,0:T(8,128)(2,1)S(1)}) fusion(f32[2,384,384]{2,1,0:T(8,128)} %param.8, bf16[384,1536]{1,0:T(8,128)(2,1)} %all-reduce.3.cloned.1.call-done, bf16[2,384,1536]{2,1,0:T(8,128)(2,1)} %param.7), kind=kOutput, calls=%fused_computation.40 | convolution fusion | flops 2724397056 | bytes 8847360 | tf_op jit(solution)/shard_map/dot_general | solution.py:17
  81.3 5.0 %reshape.26 = f32[12,32,48,32]{3,2,1,0:T(8,128)} reshape(bf16[384,1536]{1,0:T(8,128)(2,1)S(1)} %get-tuple-element.6) | data formatting | bytes 3538944 | tf_op jit(solution)/shard_map/reshape | solution.py:11
  86.3 10.8 %copy.8 = f32[12,32,48,32]{3,2,1,0:T(8,128)} copy(f32[12,32,48,32]{1,2,3,0:T(8,128)} %bitcast.65) | data formatting | bytes 4718592 | tf_op jit(solution)/shard_map/transpose | solution.py:12
  97.1 7.7 %reshape.27 = f32[384,1536]{1,0:T(8,128)} reshape(f32[12,32,48,32]{3,2,1,0:T(8,128)} %copy.8) | data formatting | bytes 4718592 | tf_op jit(solution)/shard_map/reshape | solution.py:12
  104.8 2.0 fusion.21
  106.9 0.0 all-gather.2.cloned.1.call-update
  106.9 0.0 all-reduce.5.cloned.1.call-start
  106.9 31.5 %all-gather.2.cloned.1.call-done = bf16[96,12288]{1,0:T(8,128)(2,1)} async-done(((bf16[96,1536]{1,0:T(8,128)(2,1)}), bf16[96,12288]{1,0:T(8,128)(2,1)}) %all-gather.2.cloned.1.call-update) | async-done | bytes 2359312 | tf_op jit(solution)/shard_map/all_gather | solution.py:51
  138.5 1.8 copy.15
  140.3 32.0 %all_to_all.13 = bf16[96,4,3072]{2,0,1:T(8,128)(2,1)S(1)} all-to-all(bf16[96,4,3072]{2,0,1:T(8,128)(2,1)S(1)} %bitcast.66), channel_id=1, replica_groups=mesh['past'=4,'second'=8] {'past'}, dimensions={1} | all-to-all | bytes 4718592 | tf_op jit(solution)/shard_map/all_to_all | solution.py:52
  172.4 2.7 convert_bitcast_fusion
  175.1 12.3 %reshape.32 = f32[12,32,96,32]{3,2,1,0:T(8,128)} reshape(f32[4,96,3072]{2,1,0:T(8,128)} %convert_bitcast_fusion) | data formatting | bytes 9437184 | tf_op jit(solution)/shard_map/convert_element_type | solution.py:55
  187.4 22.5 %copy.10 = f32[12,32,96,32]{3,2,1,0:T(8,128)} copy(f32[12,32,96,32]{1,2,3,0:T(8,128)} %bitcast.64) | data formatting | bytes 9437184 | tf_op jit(solution)/shard_map/convert_element_type | solution.py:55
  209.9 14.6 %reshape.31 = f32[384,3072]{1,0:T(8,128)} reshape(f32[12,32,96,32]{3,2,1,0:T(8,128)} %copy.10) | data formatting | bytes 9437184 | tf_op jit(solution)/shard_map/convert_element_type | solution.py:55
  224.4 0.0 copy-start.1
  224.5 10.7 %convolution_convert_fusion = bf16[384,1536]{1,0:T(8,128)(2,1)} fusion(bf16[3072,1536]{1,0:T(8,128)(2,1)} %param.5, f32[384,3072]{1,0:T(8,128)} %reshape.31, bf16[2,384,3072]{2,1,0:T(8,128)(2,1)} %param.6), kind=kOutput, calls=%fused_computation.9 | convolution fusion | flops 3628007424 | bytes 17694720 | tf_op jit(solution)/shard_map/dot_general | solution.py:42
  235.2 0.0 all-reduce.5.cloned.1.call-update
  235.2 52.3 %all-reduce.5.cloned.1.call-done = bf16[384,1536]{1,0:T(8,128)(2,1)} async-done(((bf16[384,1536]{1,0:T(8,128)(2,1)}), bf16[384,1536]{1,0:T(8,128)(2,1)}) %all-reduce.5.cloned.1.call-update) | async-done | bytes 1179664 | tf_op jit(solution)/shard_map/psum | solution.py:43
  287.5 0.0 copy-done.1
  287.5 6.1 %fusion.5 = bf16[1,384,1536]{2,1,0:T(8,128)(2,1)S(1)} fusion(bf16[384,1536]{1,0:T(8,128)(2,1)} %all-reduce.5.cloned.1.call-done, bf16[2,384,1536]{2,1,0:T(8,128)(2,1)S(1)} %copy-done.1, f32[2,384,384]{2,1,0:T(8,128)} %param.8), kind=kOutput, calls=%fused_computation.11 | convolution fusion | flops 2723807232 | bytes 6488064 | tf_op jit(solution)/shard_map/dot_general | solution.py:17
  293.6 1.6 pad_maximum_fusion
Async XLA Ops:
  6.5 9.3 %copy-start = (f32[32,32]{1,0:T(8,128)S(1)}, f32[32,32]{1,0:T(8,128)}, u32[]{:S(2)}) copy-start(f32[32,32]{1,0:T(8,128)} %param.9) | copy-start | bytes 12292
  6.5 66.5 %all-reduce.3.cloned.1.call-start = ((), (), s32[]{:S(2)}) async-start(), calls=%async_computation.1 | async-start | bytes 2359296 | tf_op jit(solution)/shard_map/psum | solution.py:43
  15.8 122.7 %all-gather.2.cloned.1.call-start = ((), (), s32[]{:S(2)}) async-start(), calls=%async_computation.2 | async-start | bytes 2654208 | tf_op jit(solution)/shard_map/all_gather | solution.py:51
  106.9 180.6 %all-reduce.5.cloned.1.call-start = ((), (), s32[]{:S(2)}) async-start(), calls=%async_computation.3 | async-start | bytes 2359296 | tf_op jit(solution)/shard_map/psum | solution.py:43
  224.4 63.0 %copy-start.1 = (bf16[2,384,1536]{2,1,0:T(8,128)(2,1)S(1)}, bf16[2,384,1536]{2,1,0:T(8,128)(2,1)}, u32[]{:S(2)}) copy-start(bf16[2,384,1536]{2,1,0:T(8,128)(2,1)} %param.7) | copy-start | bytes 7077892
Sparse Core Ops, SparseCore 0:
  15.9 57.0 all-reduce.2
  107.0 31.4 all-gather.1
  235.3 52.1 all-reduce.4
where the time goes:
time: 303 us; the launch traced here: 302 us
  waiting for transfers between devices  130 us (43%)
  local copies, waits for them, and re-layouts  86.1 us (28%)
  matrix products  34.3 us (11%)
  blocking collectives  32 us (11%)
  between operations  13.2 us (4%)
  other arithmetic  6.39 us (2%)
    psum x2, waiting for transfers between devices, advance(): lax.psum(partial_value.astype(jnp.bfloat16), 'past').astype(jnp.float32)  98.1 us
    convert_element_type x3, local copies, waits for them, and re-layouts, per_device(): orbital_flip(gathered, orbitals).astype(jnp.float32)  49.4 us
    all_to_all x1, blocking collectives, per_device(): lax.all_to_all(wide_band, 'past', split_axis=1, concat_axis=0, tiled=True)  32 us
    all_gather x1, waiting for transfers between devices, per_device(): wide_band = lax.all_gather(own_rows, 'second', axis=1, tiled=True)  31.5 us
    dot_general x2, matrix products, advance(): jnp.dot(memory_row, resident, preferred_element_type=jnp.float32)  19.9 us
    dot_general x2, matrix products, solve_front(): jnp.dot(inverse_block, source, precision=lax.Precision.HIGHEST, preferred...  14.3 us
    mul x2, local copies, waits for them, and re-layouts, self_energy(): blocks * pair_coupling[None, :, None, :]  11.3 us
    transpose x1, local copies, waits for them, and re-layouts, orbital_flip(): return blocks.transpose(0, 3, 2, 1).reshape(row_count, col_count)  10.8 us
  transfers between devices with their start and end apart: 3, of which 3 were waited for; matrix products, arithmetic and copies ran while one was open for 4% of the time, Pallas kernels for 0%

commit v1 on v0

--- a/solution.py
+++ b/solution.py
@@ -1,9 +1,16 @@
+import functools
+
 import jax
 import jax.numpy as jnp
 from jax import lax
+from jax.experimental import pallas as pl
+from jax.experimental.pallas import tpu as pltpu
 from jax.sharding import PartitionSpec as P
 
 step_size = 0.5
+MESH = pl.DeviceIdType.MESH
+LANES = 128
+CORES = 2
 
 
 def orbital_flip(block, orbitals):
@@ -35,14 +42,13 @@
     )
 
 
-def per_device(resident, memory, previous, inverse_part, pair_coupling):
+def per_device_plain(resident, memory, previous, inverse_part, pair_coupling):
     past_count = lax.axis_size("past")
 
     def advance(memory_row, front_index):
         partial_value = jnp.dot(memory_row, resident, preferred_element_type=jnp.float32)
         summed = lax.psum(partial_value.astype(jnp.bfloat16), "past").astype(jnp.float32)
-        prior_cols = previous[front_index]
-        return solve_front(summed, prior_cols, inverse_part[front_index])
+        return solve_front(summed, previous[front_index], inverse_part[front_index])
 
     front_one = advance(memory[0], 0)
     energy_one = self_energy(front_one, pair_coupling)
@@ -50,17 +56,325 @@
     own_rows = lax.dynamic_slice_in_dim(energy_one, lax.axis_index("past") * band, band, 0)
     wide_band = lax.all_gather(own_rows, "second", axis=1, tiled=True)
     gathered = lax.all_to_all(wide_band, "past", split_axis=1, concat_axis=0, tiled=True)
-    orbitals = pair_coupling.shape[0]
     memory_next = (
-        memory[1].astype(jnp.float32) + orbital_flip(gathered, orbitals).astype(jnp.float32)
+        memory[1].astype(jnp.float32)
+        + orbital_flip(gathered, pair_coupling.shape[0]).astype(jnp.float32)
     ).astype(jnp.bfloat16)
     front_two = advance(memory_next, 1)
     return jnp.stack([front_one, front_two])
 
 
+def flip_bit(index, mask):
+    bit = 1
+    while bit <= mask:
+        if mask & bit:
+            index = index + bit - 2 * bit * ((index // bit) % 2)
+        bit *= 2
+    return index
+
+
+def flip_tile(tile, orbitals):
+    size = tile.shape[0]
+    turned = tile.T
+    row_block = lax.broadcasted_iota(jnp.int32, tile.shape, 0) // orbitals
+    col_block = lax.broadcasted_iota(jnp.int32, tile.shape, 1) // orbitals
+    count = size // orbitals
+    lag = (row_block - col_block + count) % count
+    out = turned
+    for d in range(1, count):
+        moved = pltpu.roll(turned, d * orbitals, axis=0)
+        moved = pltpu.roll(moved, size - d * orbitals, axis=1)
+        out = jnp.where(lag == d, moved, out)
+    return out
+
+
+def kernel(
+    n, resident, memory, previous, inverse, coupling, out,
+    res, mem0, mem1, prev, inv, acc, sbuf, rsum, gbuf, front, ebuf, rbuf,
+    res_sem, mem0_sem, mem1_sem, small_sem, out_sem,
+    rs_send, rs_recv, ag_send, ag_recv,
+    up_send, down_send, line_recv, plane_send, plane_recv, core_send, core_recv,
+):
+    me = lax.axis_index("past")
+    second = lax.axis_index("second")
+    place, core = second // CORES, second % CORES
+    partner = place * CORES + 1 - core
+    rows, share = sbuf.shape[2], sbuf.shape[3]
+    orbitals = coupling.shape[0]
+    highest = lax.Precision.HIGHEST
+
+    def columns(index):
+        return pl.ds(pl.multiple_of(index * share, LANES), share)
+
+    load_mem0 = pltpu.make_async_copy(memory.at[0], mem0, mem0_sem)
+    load_mem0.start()
+    def load_res(q):
+        return pltpu.make_async_copy(resident.at[:, columns(q)], res.at[q], res_sem.at[q])
+    for i in range(n - 1, -1, -1):
+        load_res(flip_bit(me, i)).start()
+    load_prev = pltpu.make_async_copy(previous.at[:, :, columns(me)], prev, small_sem.at[0])
+    load_inv = pltpu.make_async_copy(inverse, inv, small_sem.at[1])
+    load_prev.start()
+    load_inv.start()
+    def load_mem1(k):
+        return pltpu.make_async_copy(memory.at[1, :, columns(k)], mem1.at[k], mem1_sem.at[k])
+    for k in range(CORES * n):
+        load_mem1(k).start()
+
+    barrier = pltpu.get_barrier_semaphore()
+    for i in range(1, n):
+        pl.semaphore_signal(barrier, inc=1, device_id={"past": flip_bit(me, i)}, device_id_type=MESH)
+    pl.semaphore_signal(barrier, inc=1, device_id={"second": partner}, device_id_type=MESH)
+    @pl.when(place > 0)
+    def _():
+        pl.semaphore_signal(barrier, inc=1, device_id={"second": second - CORES}, device_id_type=MESH)
+    @pl.when(place < n - 1)
+    def _():
+        pl.semaphore_signal(barrier, inc=1, device_id={"second": second + CORES}, device_id_type=MESH)
+    has_lower, has_upper = (place + n - 1) // n, (2 * (n - 1) - place) // n
+    pl.semaphore_wait(barrier, n + has_lower + has_upper)
+
+    def remote(src, dst, send, recv, **where):
+        return pltpu.make_async_remote_copy(
+            src_ref=src, dst_ref=dst, send_sem=send, recv_sem=recv,
+            device_id=where, device_id_type=MESH,
+        )
+
+    def scatter(f, q):
+        return remote(sbuf.at[f, q], rsum.at[f, me], rs_send.at[f, q], rs_recv.at[f, me], past=q)
+
+    def scatter_arrival(f, q):
+        return remote(sbuf.at[f, q], rsum.at[f, q], rs_send.at[f, q], rs_recv.at[f, q], past=q)
+
+    def gather(f, q):
+        return remote(gbuf.at[f], out.at[f, :, columns(me)], ag_send.at[f, q], ag_recv.at[f, me], past=q)
+
+    def gather_arrival(f, q):
+        return remote(gbuf.at[f], out.at[f, :, columns(q)], ag_send.at[f, q], ag_recv.at[f, q], past=q)
+
+    def keep(f):
+        return pltpu.make_async_copy(gbuf.at[f], out.at[f, :, columns(me)], out_sem.at[f])
+
+    def finish_front(f, own):
+        total = own
+        for i in range(1, n):
+            q = flip_bit(me, i)
+            scatter_arrival(f, q).wait_recv()
+            total = total + rsum[f, q].astype(jnp.float32)
+        source = prev[f].astype(jnp.float32) - step_size * total
+        solved = source + jnp.dot(
+            inv[f], source, precision=highest, preferred_element_type=jnp.float32
+        )
+        gbuf[f] = solved.astype(jnp.bfloat16)
+
+    load_mem0.wait()
+    own = None
+    for i in range(n - 1, -1, -1):
+        q = flip_bit(me, i)
+        load_res(q).wait()
+        term = jnp.dot(mem0[...], res[q], preferred_element_type=jnp.float32)
+        if i:
+            sbuf[0, q] = term.astype(jnp.bfloat16)
+            scatter(0, q).start()
+        else:
+            acc[me] = term
+    load_prev.wait()
+    load_inv.wait()
+    finish_front(0, acc[me])
+
+    width = LANES
+    spread = (
+        lax.broadcasted_iota(jnp.int32, (width, orbitals), 0) % orbitals
+        == lax.broadcasted_iota(jnp.int32, (width, orbitals), 1)
+    ).astype(jnp.float32)
+    half = lax.dot_general(spread, coupling[...], (((1,), (1,)), ((), ())),
+                           precision=highest, preferred_element_type=jnp.float32)
+    weight = lax.dot_general(half, spread, (((1,), (1,)), ((), ())),
+                             precision=highest, preferred_element_type=jnp.float32)
+    front[...] = gbuf[0].astype(jnp.float32)
+    for r in range(rows // width):
+        for s in range(share // width):
+            at = (slice(r * width, (r + 1) * width), slice(s * width, (s + 1) * width))
+            values = front[at]
+            mirror = flip_tile(values, orbitals)
+            ebuf[(place,) + at] = (mirror * mirror * values * weight).astype(jnp.bfloat16)
+
+    def up(j):
+        return remote(ebuf.at[j], ebuf.at[j], up_send.at[j], line_recv.at[j], second=second + CORES)
+
+    def down(j):
+        return remote(ebuf.at[j], ebuf.at[j], down_send.at[j], line_recv.at[j], second=second - CORES)
+
+    def to_owner(j):
+        return remote(ebuf.at[j], rbuf.at[core, me], plane_send.at[j], plane_recv.at[me], past=j)
+
+    def owner_arrival(q):
+        return remote(ebuf.at[q], rbuf.at[core, q], plane_send.at[q], plane_recv.at[q], past=q)
+
+    def to_partner_own():
+        return remote(ebuf.at[me], rbuf.at[core, me], core_send.at[me], core_recv.at[me], second=partner)
+
+    def to_partner(q):
+        return remote(rbuf.at[core, q], rbuf.at[core, q], core_send.at[q], core_recv.at[q], second=partner)
+
+    def partner_arrival(q):
+        return remote(rbuf.at[1 - core, q], rbuf.at[1 - core, q], core_send.at[q], core_recv.at[q], second=partner)
+
+    def deliver(j):
+        @pl.when(j != me)
+        def _():
+            to_owner(j).start()
+        @pl.when(j == me)
+        def _():
+            to_partner_own().start()
+
+    @pl.when(place < n - 1)
+    def _():
+        up(place).start()
+    @pl.when(place > 0)
+    def _():
+        down(place).start()
+    deliver(place)
+    for k in range(1, n):
+        @pl.when(place >= k)
+        def _():
+            j = place - k
+            down(j).wait_recv()
+            @pl.when(place < n - 1)
+            def _():
+                up(j).start()
+            deliver(j)
+        @pl.when(place + k < n)
+        def _():
+            j = place + k
+            up(j).wait_recv()
+            @pl.when(place > 0)
+            def _():
+                down(j).start()
+            deliver(j)
+    keep(0).start()
+    for i in range(n - 1, 0, -1):
+        gather(0, flip_bit(me, i)).start()
+    for k in range(CORES * n):
+        load_mem1(k).wait()
+
+    def add_energy(k, energy):
+        mem1[k] = (mem1[k].astype(jnp.float32) + energy.astype(jnp.float32)).astype(jnp.bfloat16)
+
+    for i in range(n):
+        q = flip_bit(me, i)
+        mine, other = core * n + q, (1 - core) * n + q
+        if i == 0:
+            add_energy(mine, ebuf[me])
+        else:
+            owner_arrival(q).wait_recv()
+            to_partner(q).start()
+            add_energy(mine, rbuf[core, q])
+        partner_arrival(q).wait_recv()
+        add_energy(other, rbuf[1 - core, q])
+
+        def term_of(c, i=i, q=q):
+            term = None
+            for k in (q, n + q):
+                part = jnp.dot(
+                    mem1[k], res[c, pl.ds(pl.multiple_of(k * share, LANES), share), :],
+                    preferred_element_type=jnp.float32,
+                )
+                term = part if term is None else term + part
+            return term if i == 0 else acc[c] + term
+
+        if i < n - 1:
+            @pl.loop(0, n)
+            def _(c):
+                acc[c] = term_of(c)
+        else:
+            for h in range(n - 1, 0, -1):
+                c = flip_bit(me, h)
+                sbuf[1, c] = term_of(c).astype(jnp.bfloat16)
+                scatter(1, c).start()
+            acc[me] = term_of(me)
+    finish_front(1, acc[me])
+    keep(1).start()
+    for i in range(n - 1, 0, -1):
+        gather(1, flip_bit(me, i)).start()
+
+    for i in range(n):
+        q = flip_bit(me, i)
+        if i == 0:
+            to_partner_own().wait_send()
+        else:
+            to_partner(q).wait_send()
+            to_owner(q).wait_send()
+            for f in range(2):
+                scatter(f, q).wait_send()
+                gather(f, q).wait_send()
+                gather_arrival(f, q).wait_recv()
+    for j in range(n):
+        @pl.when((place < n - 1) & (place >= j))
+        def _():
+            up(j).wait_send()
+        @pl.when((place > 0) & (place <= j))
+        def _():
+            down(j).wait_send()
+    for f in range(2):
+        keep(f).wait()
+
+
+def per_device(resident, memory, previous, inverse_part, pair_coupling, n):
+    depth, cols = resident.shape
+    rows = memory.shape[1]
+    share = cols // n
+    bf16, f32 = jnp.bfloat16, jnp.float32
+    dma = pltpu.SemaphoreType.DMA
+    hbm = pl.BlockSpec(memory_space=pl.ANY)
+    return pl.pallas_call(
+        functools.partial(kernel, n),
+        out_shape=jax.ShapeDtypeStruct(previous.shape, bf16),
+        in_specs=[hbm, hbm, hbm, hbm, pl.BlockSpec(memory_space=pltpu.VMEM)],
+        out_specs=hbm,
+        scratch_shapes=[
+            pltpu.VMEM((n, depth, share), bf16),
+            pltpu.VMEM((rows, depth), bf16),
+            pltpu.VMEM((CORES * n, rows, share), bf16),
+            pltpu.VMEM((2, rows, share), bf16),
+            pltpu.VMEM((2, rows, rows), f32),
+            pltpu.VMEM((n, rows, share), f32),
+            pltpu.VMEM((2, n, rows, share), bf16),
+            pltpu.VMEM((2, n, rows, share), bf16),
+            pltpu.VMEM((2, rows, share), bf16),
+            pltpu.VMEM((rows, share), f32),
+            pltpu.VMEM((n, rows, share), bf16),
+            pltpu.VMEM((CORES, n, rows, share), bf16),
+            dma((n,)), dma, dma((CORES * n,)), dma((2,)), dma((2,)),
+            dma((2, n)), dma((2, n)), dma((2, n)), dma((2, n)),
+            dma((n,)), dma((n,)), dma((n,)), dma((n,)), dma((n,)), dma((n,)), dma((n,)),
+        ],
+        compiler_params=pltpu.CompilerParams(
+            collective_id=0, has_side_effects=True, vmem_limit_bytes=56 * 1024 * 1024
+        ),
+    )(resident, memory, previous, inverse_part, pair_coupling)
+
+
 def solution(mesh):
+    past, second = mesh.shape["past"], mesh.shape["second"]
     in_specs = (P("past", "second"), P(None, None, "past"), P(None, None, "second"), P(), P())
     out_specs = P(None, None, "second")
+
+    def body(resident, memory, previous, inverse_part, pair_coupling):
+        depth, cols = resident.shape
+        orbitals = pair_coupling.shape[0]
+        fits = (
+            cols % (past * LANES) == 0
+            and past & (past - 1) == 0
+            and second == CORES * past
+            and depth == CORES * cols
+            and memory.shape[1] % LANES == 0
+            and LANES % orbitals == 0
+        )
+        if fits:
+            return per_device(resident, memory, previous, inverse_part, pair_coupling, past)
+        return per_device_plain(resident, memory, previous, inverse_part, pair_coupling)
+
     return jax.shard_map(
-        per_device, mesh=mesh, in_specs=in_specs, out_specs=out_specs, check_vma=False
+        body, mesh=mesh, in_specs=in_specs, out_specs=out_specs, check_vma=False
     )

time: 303 us -> 109 us (0.36)
  waiting for transfers between devices: 130 us -> 0 us
  Pallas kernels: 0 us -> 106 us
  local copies, waits for them, and re-layouts: 86.1 us -> 3.22 us
  matrix products: 34.3 us -> 0 us
  blocking collectives: 32 us -> 0 us
  between operations: 13.2 us -> 0.01 us
  other arithmetic: 6.39 us -> 0 us
    pallas_call x0 -> x1, Pallas kernels: none -> 106 us  [per_device(): pl.pallas_call(functools.partial(kernel, n), out_shape=jax.ShapeDtypeStru...]
    psum x2 -> x0, waiting for transfers between devices: 98.1 us -> none  [advance(): lax.psum(partial_value.astype(jnp.bfloat16), 'past').astype(jnp.float32)]
    convert_element_type x3 -> x0, local copies, waits for them, and re-layouts: 49.4 us -> none  [per_device(): orbital_flip(gathered, orbitals).astype(jnp.float32)]
    dot_general x4 -> x0, matrix products: 34.3 us -> none  [the longest x2 19.9 us: advance(): jnp.dot(memory_row, resident, preferred_element_type=jnp.float32)]
    all_to_all x1 -> x0, blocking collectives: 32 us -> none  [per_device(): lax.all_to_all(wide_band, 'past', split_axis=1, concat_axis=0, tiled=True)]
    all_gather x1 -> x0, waiting for transfers between devices: 31.5 us -> none  [per_device(): wide_band = lax.all_gather(own_rows, 'second', axis=1, tiled=True)]
    reshape x2 -> x0, local copies, waits for them, and re-layouts: 12.7 us -> none  [the longest x1 7.73 us: orbital_flip(): return blocks.transpose(0, 3, 2, 1).reshape(row_count, col_count)]
    mul x2 -> x0, local copies, waits for them, and re-layouts: 11.3 us -> none  [self_energy(): blocks * pair_coupling[None, :, None, :]]
  transfers between devices with their start and end apart: 3 -> 0, of which waited for: 3 -> 0; matrix products, arithmetic and copies ran while one was open for 4% -> 0% of each run, Pallas kernels for 0% -> 0%
where the time goes in v1:
time: 109 us
  Pallas kernels  106 us (97%)
  local copies, waits for them, and re-layouts  3.22 us (3%)
    pallas_call x1, Pallas kernels, per_device(): pl.pallas_call(functools.partial(kernel, n), out_shape=jax.ShapeDtypeStru...  106 us
    unnamed x1, local copies, waits for them, and re-layouts  3.22 us

profile of v1, /device:TPU:0, one launch (start us, length us, event | category | flops | bytes accessed | tf_op | source)
XLA Modules:
  0.0 108.9 jit_solution(15062590106138103223)
XLA Ops:
  0.0 105.6 %shard_map.55 = bf16[2,384,1536]{2,1,0:T(8,128)(2,1)} custom-call(bf16[3072,1536]{1,0:T(8,128)(2,1)} %resident.1, bf16[2,384,3072]{2,1,0:T(8,128)(2,1)} %memory.1, bf16[2,384,1536]{2,1,0:T(8,128)(2,1)} %previous.1, f32[2,384,384]{2,1,0:T(8,128)} %inverse.1, f32[32,32]{1,0:T(8,128)} %coupling.1), custom_call_target="tpu_custom_call" | custom-call | tf_op jit(solution)/shard_map/pallas_call | solution.py:330
  105.6 3.2 %copy.7 = bf16[2,384,1536]{2,1,0:T(8,128)(2,1)} copy(bf16[2,384,1536]{2,1,0:T(8,128)(2,1)} %shard_map.55) | data formatting | bytes 4718592

commit v2 on v0

--- a/solution.py
+++ b/solution.py
@@ -1,9 +1,16 @@
+import functools
+
 import jax
 import jax.numpy as jnp
 from jax import lax
+from jax.experimental import pallas as pl
+from jax.experimental.pallas import tpu as pltpu
 from jax.sharding import PartitionSpec as P
 
 step_size = 0.5
+MESH = pl.DeviceIdType.MESH
+LANES = 128
+CORES = 2
 
 
 def orbital_flip(block, orbitals):
@@ -35,14 +42,13 @@
     )
 
 
-def per_device(resident, memory, previous, inverse_part, pair_coupling):
+def per_device_plain(resident, memory, previous, inverse_part, pair_coupling):
     past_count = lax.axis_size("past")
 
     def advance(memory_row, front_index):
         partial_value = jnp.dot(memory_row, resident, preferred_element_type=jnp.float32)
         summed = lax.psum(partial_value.astype(jnp.bfloat16), "past").astype(jnp.float32)
-        prior_cols = previous[front_index]
-        return solve_front(summed, prior_cols, inverse_part[front_index])
+        return solve_front(summed, previous[front_index], inverse_part[front_index])
 
     front_one = advance(memory[0], 0)
     energy_one = self_energy(front_one, pair_coupling)
@@ -50,17 +56,366 @@
     own_rows = lax.dynamic_slice_in_dim(energy_one, lax.axis_index("past") * band, band, 0)
     wide_band = lax.all_gather(own_rows, "second", axis=1, tiled=True)
     gathered = lax.all_to_all(wide_band, "past", split_axis=1, concat_axis=0, tiled=True)
-    orbitals = pair_coupling.shape[0]
     memory_next = (
-        memory[1].astype(jnp.float32) + orbital_flip(gathered, orbitals).astype(jnp.float32)
+        memory[1].astype(jnp.float32)
+        + orbital_flip(gathered, pair_coupling.shape[0]).astype(jnp.float32)
     ).astype(jnp.bfloat16)
     front_two = advance(memory_next, 1)
     return jnp.stack([front_one, front_two])
 
 
+def flip_bit(index, mask):
+    bit = 1
+    while bit <= mask:
+        if mask & bit:
+            index = index + bit - 2 * bit * ((index // bit) % 2)
+        bit *= 2
+    return index
+
+
+def flip_tile(tile, orbitals):
+    size = tile.shape[0]
+    turned = tile.T
+    row_block = lax.broadcasted_iota(jnp.int32, tile.shape, 0) // orbitals
+    col_block = lax.broadcasted_iota(jnp.int32, tile.shape, 1) // orbitals
+    count = size // orbitals
+    lag = (row_block - col_block + count) % count
+    out = turned
+    for d in range(1, count):
+        moved = pltpu.roll(turned, d * orbitals, axis=0)
+        moved = pltpu.roll(moved, size - d * orbitals, axis=1)
+        out = jnp.where(lag == d, moved, out)
+    return out
+
+
+def kernel(
+    n, resident, memory, previous, inverse, coupling, out,
+    res, mem0, mem1, prev, inv, split, acc, sbuf, rsum, gbuf, front, ebuf, rbuf,
+    res_sem, mem0_sem, mem1_sem, small_sem, out_sem,
+    rs_send, rs_recv, ag_send, ag_recv,
+    up_send, down_send, line_recv, plane_send, plane_recv, core_send, core_recv,
+):
+    me = lax.axis_index("past")
+    second = lax.axis_index("second")
+    place, core = second // CORES, second % CORES
+    partner = place * CORES + 1 - core
+    rows, share = front.shape
+    orbitals = coupling.shape[0]
+    half = rows // 2
+    pieces = rows // LANES
+    highest = lax.Precision.HIGHEST
+    near = (flip_bit(me, 1), flip_bit(me, 2))
+    far = flip_bit(me, 3)
+
+    def columns(index):
+        return pl.ds(pl.multiple_of(index * share, LANES), share)
+
+    def part(h):
+        return pl.ds(h * half, half)
+
+    load_mem0 = pltpu.make_async_copy(memory.at[0], mem0, mem0_sem)
+    load_mem0.start()
+    def load_res(q):
+        return pltpu.make_async_copy(resident.at[:, columns(q)], res.at[q], res_sem.at[q])
+    for q in (far, *near, me):
+        load_res(q).start()
+    load_prev = pltpu.make_async_copy(previous.at[:, :, columns(me)], prev, small_sem.at[0])
+    load_inv = pltpu.make_async_copy(inverse, inv, small_sem.at[1])
+    load_prev.start()
+    load_inv.start()
+    def load_mem1(k):
+        return pltpu.make_async_copy(memory.at[1, :, columns(k)], mem1.at[k], mem1_sem.at[k])
+    for k in range(CORES * n):
+        load_mem1(k).start()
+
+    barrier = pltpu.get_barrier_semaphore()
+    for q in (far, *near):
+        pl.semaphore_signal(barrier, inc=1, device_id={"past": q}, device_id_type=MESH)
+    pl.semaphore_signal(barrier, inc=1, device_id={"second": partner}, device_id_type=MESH)
+    @pl.when(place > 0)
+    def _():
+        pl.semaphore_signal(barrier, inc=1, device_id={"second": second - CORES}, device_id_type=MESH)
+    @pl.when(place < n - 1)
+    def _():
+        pl.semaphore_signal(barrier, inc=1, device_id={"second": second + CORES}, device_id_type=MESH)
+    has_lower, has_upper = (place + n - 1) // n, (2 * (n - 1) - place) // n
+    pl.semaphore_wait(barrier, n + has_lower + has_upper)
+
+    def remote(src, dst, send, recv, **where):
+        return pltpu.make_async_remote_copy(
+            src_ref=src, dst_ref=dst, send_sem=send, recv_sem=recv,
+            device_id=where, device_id_type=MESH,
+        )
+
+    def scatter(f, link, m):
+        return remote(sbuf.at[f, link, m], rsum.at[f, link, m], rs_send.at[f, link, m],
+                      rs_recv.at[f, link, m], past=near[link])
+
+    def reduce_scatter(f, term):
+        value = term(far)
+        for link in range(2):
+            sbuf[f, link, 0] = value[link * half:(link + 1) * half].astype(jnp.bfloat16)
+            scatter(f, link, 0).start()
+        for link in range(2):
+            q = near[link]
+            acc[q] = term(q)
+            sbuf[f, link, 1] = acc[q, part(link), :].astype(jnp.bfloat16)
+            scatter(f, link, 1).start()
+        for link in range(2):
+            other = 1 - link
+            scatter(f, other, 0).wait_recv()
+            sbuf[f, link, 2] = (
+                acc[near[link], part(other), :] + rsum[f, other, 0].astype(jnp.float32)
+            ).astype(jnp.bfloat16)
+            scatter(f, link, 2).start()
+        acc[me] = term(me)
+
+    def finish_front(f):
+        for link in range(2):
+            scatter(f, link, 1).wait_recv()
+            scatter(f, link, 2).wait_recv()
+        for h in range(2):
+            total = (
+                acc[me, part(h), :]
+                + rsum[f, h, 1].astype(jnp.float32)
+                + rsum[f, 1 - h, 2].astype(jnp.float32)
+            )
+            front[part(h), :] = prev[f, part(h), :].astype(jnp.float32) - step_size * total
+        source = front[...]
+        high = source.astype(jnp.bfloat16)
+        low = (source - high.astype(jnp.float32)).astype(jnp.bfloat16)
+        dot = functools.partial(jnp.dot, preferred_element_type=jnp.float32)
+        moved = dot(split[f, 0], high) + (dot(split[f, 0], low) + dot(split[f, 1], high))
+        gbuf[f] = (source + moved).astype(jnp.bfloat16)
+
+    def gather(f, link, m):
+        if m < 2:
+            h, q = (link, 1 - link)[m], me
+            src = gbuf.at[f, part(h), :]
+        else:
+            h, q = 1 - link, near[1 - link]
+            src = out.at[f, part(h), columns(q)]
+        return remote(src, out.at[f, part(h), columns(q)], ag_send.at[f, link, m],
+                      ag_recv.at[f, link, m], past=near[link])
+
+    def gather_arrival(f, link, m):
+        h = link if m == 0 else 1 - link
+        q = far if m == 2 else near[link]
+        ref = out.at[f, part(h), columns(q)]
+        return remote(ref, ref, ag_send.at[f, link, m], ag_recv.at[f, link, m], past=near[link])
+
+    def keep(f):
+        return pltpu.make_async_copy(gbuf.at[f], out.at[f, :, columns(me)], out_sem.at[f])
+
+    def gather_own(f):
+        for m in range(2):
+            for link in range(2):
+                gather(f, link, m).start()
+        keep(f).start()
+
+    def gather_relay(f):
+        for link in range(2):
+            gather_arrival(f, 1 - link, 0).wait_recv()
+            gather(f, link, 2).start()
+
+    load_mem0.wait()
+    def first_term(q):
+        load_res(q).wait()
+        return jnp.dot(mem0[...], res[q], preferred_element_type=jnp.float32)
+    reduce_scatter(0, first_term)
+
+    load_prev.wait()
+    load_inv.wait()
+    for f in range(2):
+        value = inv[f]
+        high = value.astype(jnp.bfloat16)
+        split[f, 0] = high
+        split[f, 1] = (value - high.astype(jnp.float32)).astype(jnp.bfloat16)
+    spread = (
+        lax.broadcasted_iota(jnp.int32, (LANES, orbitals), 0) % orbitals
+        == lax.broadcasted_iota(jnp.int32, (LANES, orbitals), 1)
+    ).astype(jnp.float32)
+    tall = lax.dot_general(spread, coupling[...], (((1,), (1,)), ((), ())),
+                           precision=highest, preferred_element_type=jnp.float32)
+    weight = lax.dot_general(tall, spread, (((1,), (1,)), ((), ())),
+                             precision=highest, preferred_element_type=jnp.float32)
+    finish_front(0)
+
+    def to_owner(s):
+        return remote(ebuf.at[s], rbuf.at[core, me, s], plane_send.at[s], plane_recv.at[me, s], past=place)
+
+    def owner_arrival(q, s):
+        return remote(ebuf.at[s], rbuf.at[core, q, s], plane_send.at[s], plane_recv.at[q, s], past=q)
+
+    for s in range(pieces):
+        for c in range(share // LANES):
+            at = (pl.ds(s * LANES, LANES), pl.ds(c * LANES, LANES))
+            values = gbuf[(0,) + at].astype(jnp.float32)
+            mirror = flip_tile(values, orbitals)
+            ebuf[s, :, pl.ds(c * LANES, LANES)] = (mirror * mirror * values * weight).astype(jnp.bfloat16)
+        @pl.when(me != place)
+        def _():
+            to_owner(s).start()
+        @pl.when(me == place)
+        def _():
+            rbuf[core, me, s] = ebuf[s]
+    gather_own(0)
+    for k in range(CORES * n):
+        load_mem1(k).wait()
+
+    def up(q, s):
+        return remote(rbuf.at[core, q, s], rbuf.at[core, q, s], up_send.at[q, s],
+                      line_recv.at[q, s], second=second + CORES)
+
+    def down(q, s):
+        return remote(rbuf.at[core, q, s], rbuf.at[core, q, s], down_send.at[q, s],
+                      line_recv.at[q, s], second=second - CORES)
+
+    def across(q, s):
+        return remote(rbuf.at[core, q, s], rbuf.at[core, q, s], core_send.at[q, s],
+                      core_recv.at[q, s], second=partner)
+
+    def across_arrival(q, s):
+        ref = rbuf.at[1 - core, q, s]
+        return remote(ref, ref, core_send.at[q, s], core_recv.at[q, s], second=partner)
+
+    def pass_on(i, s):
+        q = (me, *near, far)[i]
+        if i:
+            @pl.when(me == place)
+            def _():
+                owner_arrival(q, s).wait_recv()
+        @pl.when(place > me)
+        def _():
+            down(q, s).wait_recv()
+        @pl.when(place < me)
+        def _():
+            up(q, s).wait_recv()
+        @pl.when((place >= me) & (place < n - 1))
+        def _():
+            up(q, s).start()
+        @pl.when((place <= me) & (place > 0))
+        def _():
+            down(q, s).start()
+        across(q, s).start()
+
+    def add_energy(q):
+        for side, is_partner in ((core, False), (1 - core, True)):
+            for s in range(pieces):
+                if is_partner:
+                    across_arrival(q, s).wait_recv()
+                at = (side * n + q, pl.ds(s * LANES, LANES))
+                mem1[at] = (
+                    mem1[at].astype(jnp.float32) + rbuf[side, q, s].astype(jnp.float32)
+                ).astype(jnp.bfloat16)
+
+    def second_term(q, c, first):
+        term = None
+        for k in (q, n + q):
+            product = jnp.dot(
+                mem1[k], res[c, pl.ds(pl.multiple_of(k * share, LANES), share), :],
+                preferred_element_type=jnp.float32,
+            )
+            term = product if term is None else term + product
+        return term if first else acc[c] + term
+
+    for i in range(n):
+        for s in range(pieces):
+            pass_on(i, s)
+            if i:
+                q = (me, *near, far)[i - 1]
+                if s == 0:
+                    add_energy(q)
+                for c in range(n):
+                    if c * pieces // n == s:
+                        acc[c] = second_term(q, c, i == 1)
+    gather_relay(0)
+    add_energy(far)
+    reduce_scatter(1, lambda c: second_term(far, c, False))
+    finish_front(1)
+    gather_own(1)
+    gather_relay(1)
+
+    for f in range(2):
+        for link in range(2):
+            for m in range(3):
+                scatter(f, link, m).wait_send()
+                gather(f, link, m).wait_send()
+                if m:
+                    gather_arrival(f, link, m).wait_recv()
+        keep(f).wait()
+    for s in range(pieces):
+        @pl.when(me != place)
+        def _():
+            to_owner(s).wait_send()
+        for q in range(n):
+            across(q, s).wait_send()
+            @pl.when((place >= me) & (place < n - 1))
+            def _():
+                up(q, s).wait_send()
+            @pl.when((place <= me) & (place > 0))
+            def _():
+                down(q, s).wait_send()
+
+
+def per_device(resident, memory, previous, inverse_part, pair_coupling, n):
+    depth, cols = resident.shape
+    rows = memory.shape[1]
+    share = cols // n
+    pieces = rows // LANES
+    bf16, f32 = jnp.bfloat16, jnp.float32
+    dma = pltpu.SemaphoreType.DMA
+    hbm = pl.BlockSpec(memory_space=pl.ANY)
+    return pl.pallas_call(
+        functools.partial(kernel, n),
+        out_shape=jax.ShapeDtypeStruct(previous.shape, bf16),
+        in_specs=[hbm, hbm, hbm, hbm, pl.BlockSpec(memory_space=pltpu.VMEM)],
+        out_specs=hbm,
+        scratch_shapes=[
+            pltpu.VMEM((n, depth, share), bf16),
+            pltpu.VMEM((rows, depth), bf16),
+            pltpu.VMEM((CORES * n, rows, share), bf16),
+            pltpu.VMEM((2, rows, share), bf16),
+            pltpu.VMEM((2, rows, rows), f32),
+            pltpu.VMEM((2, 2, rows, rows), bf16),
+            pltpu.VMEM((n, rows, share), f32),
+            pltpu.VMEM((2, 2, 3, rows // 2, share), bf16),
+            pltpu.VMEM((2, 2, 3, rows // 2, share), bf16),
+            pltpu.VMEM((2, rows, share), bf16),
+            pltpu.VMEM((rows, share), f32),
+            pltpu.VMEM((pieces, LANES, share), bf16),
+            pltpu.VMEM((CORES, n, pieces, LANES, share), bf16),
+            dma((n,)), dma, dma((CORES * n,)), dma((2,)), dma((2,)),
+            dma((2, 2, 3)), dma((2, 2, 3)), dma((2, 2, 3)), dma((2, 2, 3)),
+            dma((n, pieces)), dma((n, pieces)), dma((n, pieces)), dma((pieces,)),
+            dma((n, pieces)), dma((n, pieces)), dma((n, pieces)),
+        ],
+        compiler_params=pltpu.CompilerParams(
+            collective_id=0, has_side_effects=True, vmem_limit_bytes=56 * 1024 * 1024
+        ),
+    )(resident, memory, previous, inverse_part, pair_coupling)
+
+
 def solution(mesh):
+    past, second = mesh.shape["past"], mesh.shape["second"]
     in_specs = (P("past", "second"), P(None, None, "past"), P(None, None, "second"), P(), P())
     out_specs = P(None, None, "second")
+
+    def body(resident, memory, previous, inverse_part, pair_coupling):
+        depth, cols = resident.shape
+        orbitals = pair_coupling.shape[0]
+        fits = (
+            cols % (past * LANES) == 0
+            and past == 2 * 2
+            and second == CORES * past
+            and depth == CORES * cols
+            and memory.shape[1] % (2 * LANES) in (0, LANES)
+            and LANES % orbitals == 0
+        )
+        if fits:
+            return per_device(resident, memory, previous, inverse_part, pair_coupling, past)
+        return per_device_plain(resident, memory, previous, inverse_part, pair_coupling)
+
     return jax.shard_map(
-        per_device, mesh=mesh, in_specs=in_specs, out_specs=out_specs, check_vma=False
+        body, mesh=mesh, in_specs=in_specs, out_specs=out_specs, check_vma=False
     )

time: 303 us -> 89 us (0.29)
  waiting for transfers between devices: 130 us -> 0 us
  Pallas kernels: 0 us -> 85.5 us
  local copies, waits for them, and re-layouts: 86.1 us -> 3.22 us
  matrix products: 34.3 us -> 0 us
  blocking collectives: 32 us -> 0 us
  between operations: 13.2 us -> 0.01 us
  other arithmetic: 6.39 us -> 0 us
    psum x2 -> x0, waiting for transfers between devices: 98.1 us -> none  [advance(): lax.psum(partial_value.astype(jnp.bfloat16), 'past').astype(jnp.float32)]
    pallas_call x0 -> x1, Pallas kernels: none -> 85.5 us  [per_device(): pl.pallas_call(functools.partial(kernel, n), out_shape=jax.ShapeDtypeStru...]
    convert_element_type x3 -> x0, local copies, waits for them, and re-layouts: 49.4 us -> none  [per_device(): orbital_flip(gathered, orbitals).astype(jnp.float32)]
    dot_general x4 -> x0, matrix products: 34.3 us -> none  [the longest x2 19.9 us: advance(): jnp.dot(memory_row, resident, preferred_element_type=jnp.float32)]
    all_to_all x1 -> x0, blocking collectives: 32 us -> none  [per_device(): lax.all_to_all(wide_band, 'past', split_axis=1, concat_axis=0, tiled=True)]
    all_gather x1 -> x0, waiting for transfers between devices: 31.5 us -> none  [per_device(): wide_band = lax.all_gather(own_rows, 'second', axis=1, tiled=True)]
    reshape x2 -> x0, local copies, waits for them, and re-layouts: 12.7 us -> none  [the longest x1 7.73 us: orbital_flip(): return blocks.transpose(0, 3, 2, 1).reshape(row_count, col_count)]
    mul x2 -> x0, local copies, waits for them, and re-layouts: 11.3 us -> none  [self_energy(): blocks * pair_coupling[None, :, None, :]]
  transfers between devices with their start and end apart: 3 -> 0, of which waited for: 3 -> 0; matrix products, arithmetic and copies ran while one was open for 4% -> 0% of each run, Pallas kernels for 0% -> 0%
where the time goes in v2:
time: 89 us; the launch traced here: 88.7 us
  Pallas kernels  85.5 us (96%)
  local copies, waits for them, and re-layouts  3.22 us (4%)
    pallas_call x1, Pallas kernels, per_device(): pl.pallas_call(functools.partial(kernel, n), out_shape=jax.ShapeDtypeStru...  85.5 us
    unnamed x1, local copies, waits for them, and re-layouts  3.22 us

profile of v2, /device:TPU:0, one launch (start us, length us, event | category | flops | bytes accessed | tf_op | source)
XLA Modules:
  0.0 88.7 jit_solution(7468571772978347217)
XLA Ops:
  0.0 85.5 %shard_map.55 = bf16[2,384,1536]{2,1,0:T(8,128)(2,1)} custom-call(bf16[3072,1536]{1,0:T(8,128)(2,1)} %resident.1, bf16[2,384,3072]{2,1,0:T(8,128)(2,1)} %memory.1, bf16[2,384,1536]{2,1,0:T(8,128)(2,1)} %previous.1, f32[2,384,384]{2,1,0:T(8,128)} %inverse.1, f32[32,32]{1,0:T(8,128)} %coupling.1), custom_call_target="tpu_custom_call" | custom-call | tf_op jit(solution)/shard_map/pallas_call | solution.py:369
  85.5 3.2 %copy.7 = bf16[2,384,1536]{2,1,0:T(8,128)(2,1)} copy(bf16[2,384,1536]{2,1,0:T(8,128)(2,1)} %shard_map.55) | data formatting | bytes 4718592

commit v3 on v2

--- a/solution.py
+++ b/solution.py
@@ -11,6 +11,7 @@
 MESH = pl.DeviceIdType.MESH
 LANES = 128
 CORES = 2
+BAND = 64
 
 
 def orbital_flip(block, orbitals):
@@ -102,7 +103,7 @@
     rows, share = front.shape
     orbitals = coupling.shape[0]
     half = rows // 2
-    pieces = rows // LANES
+    pieces = rows // BAND
     highest = lax.Precision.HIGHEST
     near = (flip_bit(me, 1), flip_bit(me, 2))
     far = flip_bit(me, 3)
@@ -247,12 +248,16 @@
     def owner_arrival(q, s):
         return remote(ebuf.at[s], rbuf.at[core, q, s], plane_send.at[s], plane_recv.at[q, s], past=q)
 
+    bands = LANES // BAND
     for s in range(pieces):
-        for c in range(share // LANES):
-            at = (pl.ds(s * LANES, LANES), pl.ds(c * LANES, LANES))
-            values = gbuf[(0,) + at].astype(jnp.float32)
-            mirror = flip_tile(values, orbitals)
-            ebuf[s, :, pl.ds(c * LANES, LANES)] = (mirror * mirror * values * weight).astype(jnp.bfloat16)
+        if s % bands == 0:
+            for c in range(share // LANES):
+                across_lanes = pl.ds(c * LANES, LANES)
+                values = gbuf[0, pl.ds(s * BAND, LANES), across_lanes].astype(jnp.float32)
+                mirror = flip_tile(values, orbitals)
+                energy = (mirror * mirror * values * weight).astype(jnp.bfloat16)
+                for u in range(bands):
+                    ebuf[s + u, :, across_lanes] = energy[u * BAND:(u + 1) * BAND]
         @pl.when(me != place)
         def _():
             to_owner(s).start()
@@ -304,7 +309,7 @@
             for s in range(pieces):
                 if is_partner:
                     across_arrival(q, s).wait_recv()
-                at = (side * n + q, pl.ds(s * LANES, LANES))
+                at = (side * n + q, pl.ds(s * BAND, BAND))
                 mem1[at] = (
                     mem1[at].astype(jnp.float32) + rbuf[side, q, s].astype(jnp.float32)
                 ).astype(jnp.bfloat16)
@@ -362,7 +367,7 @@
     depth, cols = resident.shape
     rows = memory.shape[1]
     share = cols // n
-    pieces = rows // LANES
+    pieces = rows // BAND
     bf16, f32 = jnp.bfloat16, jnp.float32
     dma = pltpu.SemaphoreType.DMA
     hbm = pl.BlockSpec(memory_space=pl.ANY)
@@ -383,8 +388,8 @@
             pltpu.VMEM((2, 2, 3, rows // 2, share), bf16),
             pltpu.VMEM((2, rows, share), bf16),
             pltpu.VMEM((rows, share), f32),
-            pltpu.VMEM((pieces, LANES, share), bf16),
-            pltpu.VMEM((CORES, n, pieces, LANES, share), bf16),
+            pltpu.VMEM((pieces, BAND, share), bf16),
+            pltpu.VMEM((CORES, n, pieces, BAND, share), bf16),
             dma((n,)), dma, dma((CORES * n,)), dma((2,)), dma((2,)),
             dma((2, 2, 3)), dma((2, 2, 3)), dma((2, 2, 3)), dma((2, 2, 3)),
             dma((n, pieces)), dma((n, pieces)), dma((n, pieces)), dma((pieces,)),

time: 89 us -> 89 us (level)
  no operation moved by 1% of the time
where the time goes in v3:
time: 89 us; the launch traced here: 88.8 us
  Pallas kernels  85.6 us (96%)
  local copies, waits for them, and re-layouts  3.22 us (4%)
    pallas_call x1, Pallas kernels, per_device(): pl.pallas_call(functools.partial(kernel, n), out_shape=jax.ShapeDtypeStru...  85.6 us
    unnamed x1, local copies, waits for them, and re-layouts  3.22 us

profile of v3, /device:TPU:0, one launch (start us, length us, event | category | flops | bytes accessed | tf_op | source)
XLA Modules:
  0.0 88.8 jit_solution(4745876134653853114)
XLA Ops:
  0.0 85.6 %shard_map.55 = bf16[2,384,1536]{2,1,0:T(8,128)(2,1)} custom-call(bf16[3072,1536]{1,0:T(8,128)(2,1)} %resident.1, bf16[2,384,3072]{2,1,0:T(8,128)(2,1)} %memory.1, bf16[2,384,1536]{2,1,0:T(8,128)(2,1)} %previous.1, f32[2,384,384]{2,1,0:T(8,128)} %inverse.1, f32[32,32]{1,0:T(8,128)} %coupling.1), custom_call_target="tpu_custom_call" | custom-call | tf_op jit(solution)/shard_map/pallas_call | solution.py:374
  85.6 3.2 %copy.7 = bf16[2,384,1536]{2,1,0:T(8,128)(2,1)} copy(bf16[2,384,1536]{2,1,0:T(8,128)(2,1)} %shard_map.55) | data formatting | bytes 4718592
